TPU v7x, 128 devices: a whole 4x4x4 slice. The times are simulated.
128 devices in a mesh: req: 16 (over x, y), exp: 8 (over z, core).
Axes of the slice: x: 4, y: 4, z: 4, core: 2. Of those that a mesh axis runs over, the one named last changes fastest.
Arguments:
- tokens: bfloat16 [16384, 2048], P(('req', 'exp')), may hold values from -6 to 6
- attn_gain: float32 [2048], replicated, may hold values from 0.1 to 1.9
- w_query: bfloat16 [2048, 2048], P(None, 'exp'), may hold values from -0.25 to 0.25
- w_key: bfloat16 [2048, 2048], P(None, 'exp'), may hold values from -0.125 to 0.125
- w_value: bfloat16 [2048, 2048], P(None, 'exp'), may hold values from -0.125 to 0.125
- w_out: bfloat16 [2048, 2048], P('exp'), may hold values from -0.375 to 0.375
- prefix_cache: bfloat16 [8, 1024, 2, 2048], P(None, 'req', None, 'exp'), may hold values from -205 to 205
- group_of: int32 [16], replicated, may hold values from 0 to 7
- lengths: int32 [16], replicated, may hold values from 1 to 1024, 10240 in all
- moe_gain: float32 [2048], replicated, may hold values from 0.1 to 1.9
- w_gate: bfloat16 [128, 2048, 512], P(('req', 'exp')), may hold values from -0.125 to 0.125
- w_up: bfloat16 [128, 2048, 512], P(('req', 'exp')), may hold values from -0.125 to 0.125
- w_down: bfloat16 [128, 512, 2048], P(('req', 'exp')), may hold values from -0.25 to 0.25
- routes: int32 [16384, 8], P(('req', 'exp')), may hold values from 0 to 63, all different within a row; in each aligned block of 128 rows (0 to 127, 128 to 255, ...) at most 18 rows name the same one
- route_weights: float32 [16384, 8], P(('req', 'exp')), may hold values from 0.1 to 0.4
Outputs:
- layer_out: bfloat16 [16384, 2048], P(('req', 'exp'))
Inputs may be any that keep to these rules, and one draw needn't show every extreme that they name: `routes`: in the rows of one device no expert is named more than 18 times.
All inputs are finite; a program needn't handle non-finite values.
Results may differ from a plain program's by a relative error of at most 0.017.
Values may be sent and summed in bfloat16 or wider, within the bound.
No kernel may reach another device: no remote copies, remote signals or barrier semaphores. Data moves between devices by JAX's collectives and lax.ppermute only.
A program may use at most 192 MiB of HBM per device.

v0:
```python
import math
import jax
import jax.numpy as jnp
from jax import lax
from jax.sharding import PartitionSpec as P

HD = 128
PREFIX = 1024


def norm_rows(values, gain):
    wide = values.astype(jnp.float32)
    return wide * lax.rsqrt(jnp.mean(wide * wide, axis=-1, keepdims=True) + 1e-05) * gain


def rotate(vectors, places):
    half = vectors.shape[-1] // 2
    freqs = 10000.0 ** (-(jnp.arange(half, dtype=jnp.float32) * 2.0) / vectors.shape[-1])
    angles = places[:, None] * freqs[None, :]
    cosine = jnp.cos(angles)[:, None, :]
    sine = jnp.sin(angles)[:, None, :]
    first = vectors[..., :half]
    second = vectors[..., half:]
    return jnp.concatenate(
        [first * cosine - second * sine, first * sine + second * cosine], axis=-1
    )


def on_device(
    tokens,
    attn_gain,
    w_query,
    w_key,
    w_value,
    w_out,
    prefix_cache,
    group_of,
    lengths,
    moe_gain,
    w_gate,
    w_up,
    w_down,
    routes,
    route_weights,
):
    rows_dev, width = tokens.shape
    exp_count = lax.axis_size("exp")
    req_count = lax.axis_size("req")
    exp_index = lax.axis_index("exp")
    req_index = lax.axis_index("req")
    local_width = w_query.shape[1]
    head_dim = HD
    local_heads = local_width // head_dim
    slot_count = rows_dev * exp_count
    normed = norm_rows(tokens, attn_gain).astype(jnp.bfloat16)
    joined = jnp.concatenate([w_query, w_key, w_value], axis=1)
    piece = lax.all_gather(normed, "exp", axis=0, tiled=True)
    count = piece.shape[0]
    mixed = jnp.dot(piece, joined, preferred_element_type=jnp.float32)
    places = (PREFIX + jnp.int32(0) + jnp.arange(count, dtype=jnp.int32)).astype(jnp.float32)
    query = rotate(mixed[:, :local_width].reshape(count, local_heads, head_dim), places).reshape(
        count, local_width
    )
    key = rotate(
        mixed[:, local_width : 2 * local_width].reshape(count, local_heads, head_dim), places
    ).reshape(count, local_width)
    projected = jnp.concatenate([query, key, mixed[:, 2 * local_width :]], axis=1).astype(
        jnp.bfloat16
    )
    outgoing = jnp.take(prefix_cache, group_of, axis=0)
    arrived = lax.all_to_all(outgoing, "req", split_axis=0, concat_axis=1, tiled=True)[0]
    prefix_len = arrived.shape[0]
    query = projected[:, :local_width].reshape(slot_count, local_heads, head_dim)
    keys = jnp.concatenate(
        [
            arrived[:, 0].reshape(prefix_len, local_heads, head_dim),
            projected[:, local_width : 2 * local_width].reshape(slot_count, local_heads, head_dim),
        ],
        axis=0,
    )
    values = jnp.concatenate(
        [
            arrived[:, 1].reshape(prefix_len, local_heads, head_dim),
            projected[:, 2 * local_width :].reshape(slot_count, local_heads, head_dim),
        ],
        axis=0,
    )
    scores = jnp.einsum(
        "qhd,khd->hqk", query, keys, preferred_element_type=jnp.float32
    ) / math.sqrt(head_dim)
    length = lengths[req_index]
    live = jnp.concatenate(
        [jnp.ones((prefix_len,), bool), jnp.arange(slot_count, dtype=jnp.int32) < length]
    )
    scores = jnp.where(live[None, None, :], scores, -1e30)
    top_score = jnp.max(scores, axis=-1, keepdims=True)
    raised = jnp.exp(scores - top_score)
    probs = (raised / jnp.sum(raised, axis=-1, keepdims=True)).astype(jnp.bfloat16)
    attn = (
        jnp.einsum("hqk,khd->qhd", probs, values, preferred_element_type=jnp.float32)
        .astype(jnp.bfloat16)
        .reshape(slot_count, local_width)
    )
    attn_out = lax.psum_scatter(
        jnp.dot(attn, w_out, preferred_element_type=jnp.float32).astype(jnp.bfloat16),
        "exp",
        scatter_dimension=0,
        tiled=True,
    ).astype(jnp.float32)
    hidden_state = (tokens.astype(jnp.float32) + attn_out).astype(jnp.bfloat16)
    normed2 = norm_rows(hidden_state, moe_gain).astype(jnp.bfloat16)
    top_count = routes.shape[1]
    experts = req_count * exp_count // 2
    capacity = 2 * max(1, rows_dev * top_count * 9 // (16 * experts))
    flat = routes.reshape(-1)
    onehot = (flat[:, None] == jnp.arange(experts, dtype=jnp.int32)[None, :]).astype(jnp.int32)
    slot = jnp.sum((jnp.cumsum(onehot, axis=0) - 1) * onehot, axis=1)
    source_row = jnp.arange(rows_dev * top_count, dtype=jnp.int32) // top_count
    buffer = (
        jnp.zeros((experts, capacity, width), jnp.bfloat16).at[flat, slot].set(normed2[source_row])
    )
    doubled = jnp.broadcast_to(buffer[:, None], (experts, 2, capacity, width)).reshape(
        2 * experts, capacity, width
    )
    rows_in = lax.all_to_all(doubled, ("req", "exp"), split_axis=0, concat_axis=0, tiled=True)
    senders, count, _ = rows_in.shape
    joined_rows = rows_in.reshape(senders * count, width)
    gate = jnp.dot(joined_rows, w_gate[0], preferred_element_type=jnp.float32)
    upper = jnp.dot(joined_rows, w_up[0], preferred_element_type=jnp.float32)
    act = (jax.nn.silu(gate) * upper).astype(jnp.bfloat16)
    part = jnp.dot(act, w_down[0], preferred_element_type=jnp.float32)
    returned = lax.all_to_all(
        part.reshape(senders, count, width).astype(jnp.bfloat16),
        ("req", "exp"),
        split_axis=0,
        concat_axis=0,
        tiled=True,
    ).astype(jnp.float32)
    combined = (
        jnp.sum(returned.reshape(experts, 2, capacity, width), axis=1)
        .astype(jnp.bfloat16)
        .astype(jnp.float32)
    )
    picked = combined[flat, slot].reshape(rows_dev, top_count, width)
    moe = jnp.sum(picked * route_weights[:, :, None], axis=1)
    place = exp_index * rows_dev + jnp.arange(rows_dev, dtype=jnp.int32)
    live_rows = place < length
    return jnp.where(live_rows[:, None], hidden_state.astype(jnp.float32) + moe, 0.0).astype(
        jnp.bfloat16
    )


def solution(mesh):
    return jax.shard_map(
        on_device,
        mesh=mesh,
        in_specs=(
            P(("req", "exp"), None),
            P(),
            P(None, "exp"),
            P(None, "exp"),
            P(None, "exp"),
            P("exp", None),
            P(None, "req", None, "exp"),
            P(),
            P(),
            P(),
            P(("req", "exp"), None, None),
            P(("req", "exp"), None, None),
            P(("req", "exp"), None, None),
            P(("req", "exp"), None),
            P(("req", "exp"), None),
        ),
        out_specs=P(("req", "exp"), None),
        check_vma=False,
    )
```

profile of v0, /device:TPU:24, one launch (start us, length us, event | category | flops | bytes accessed | tf_op | source)
XLA Modules:
  0.0 606.7 jit_solution(18141215170195101366)
XLA Ops:
  10.7 3.7 gather_fusion
  17.0 7.2 %all-to-all-start = ((bf16[16,64,2,256]{3,2,1,0:T(2,128)(2,1)}), bf16[16,64,2,256]{3,2,1,0:T(2,128)(2,1)S(1)}, u32[]{:S(2)}, u32[]{:S(2)}) async-start(bf16[16,64,2,256]{3,2,1,0:T(2,128)(2,1)} %broadcast_select_fusion), calls=%async_computation | async-start | bytes 2097152 | tf_op jit(solution)/shard_map/all_to_all | solution.py:71
  28.8 10.1 %all-to-all-done = bf16[16,64,2,256]{3,2,1,0:T(2,128)(2,1)S(1)} async-done(((bf16[16,64,2,256]{3,2,1,0:T(2,128)(2,1)}), bf16[16,64,2,256]{3,2,1,0:T(2,128)(2,1)S(1)}, u32[]{:S(2)}, u32[]{:S(2)}) %all-to-all-start) | async-done | bytes 1048608 | tf_op jit(solution)/shard_map/all_to_all | solution.py:71
  44.5 6.7 %fusion.10 = f32[1024,768]{0,1:T(8,128)S(1)} fusion(bf16[1024,2048]{1,0:T(8,128)(2,1)} %all-gather.2.cloned.1.call-done, bf16[2048,256]{1,0:T(8,128)(2,1)} %param.19, bf16[2048,256]{1,0:T(8,128)(2,1)} %param.18, bf16[2048,256]{1,0:T(8,128)(2,1)} %param.17), kind=kOutput, calls=%fused_computation.23 | convolution fusion | flops 3230662656 | bytes 10485760 | tf_op jit(solution)/shard_map/dot_general | solution.py:59
  65.1 3.9 subtract_convert_fusion.1
  69.0 10.8 %fusion.53 = (f32[2,1024]{1,0:T(2,128)S(1)}, f32[2,1024,2048]{2,1,0:T(8,128)}) fusion(pred[2048]{0:T(1024)(128)(4,1)S(1)} %concatenate.28, bf16[1024,2,64]{2,0,1:T(8,128)(2,1)} %get-tuple-element.13, bf16[1024,2,64]{2,0,1:T(8,128)(2,1)} %get-tuple-element.14, bf16[1024,2,128]{2,0,1:T(8,128)(2,1)} %copy.92, bf16[1024,2,64]{2,0,1:T(8,128)(2,1)} %get-tuple-element.6, ...), kind=kOutput, calls=%fused_computation.105 | convolution fusion | flops 1094715392 | bytes 18360320 | tf_op jit(solution)/shard_map/sub | solution.py:97
  79.9 8.8 %fusion.24 = bf16[2,128,1024]{2,1,0:T(8,128)(2,1)S(1)} fusion(f32[2,1024,2048]{2,1,0:T(8,128)} %get-tuple-element.25, f32[2,1024]{1,0:T(2,128)S(1)} %get-tuple-element.24, bf16[1024,2,128]{0,2,1:T(8,128)(2,1)S(1)} %bitcast.62, bf16[1024,2,128]{0,2,1:T(8,128)(2,1)S(1)} %bitcast.61), kind=kOutput, calls=%fused_computation.43 | convolution fusion | flops 1084489728 | bytes 18358272 | tf_op jit(solution)/shard_map/hqk,khd->qhd/dot_general | solution.py:100
  92.4 18.0 %reduce-window.6 = s32[64,8,128]{2,1,0:T(8,128)S(1)} reduce-window(s32[64,8,128]{2,1,0:T(8,128)S(1)} %fusion.39, s32[]{:T(128)} %constant.39.clone.1), window={size=1x1x128 pad=0_0x0_0x127_0}, to_apply=%region_4.5 | reduce-window | flops 8323072 | bytes 524292 | tf_op jit(solution)/shard_map/reduce-window
  111.3 19.1 %reduce-scatter.2.cloned.1.call-done = bf16[128,2048]{1,0:T(8,128)(2,1)} async-done(((bf16[1024,2048]{1,0:T(8,128)(2,1)}), bf16[128,2048]{1,0:T(8,128)(2,1)}) %reduce-scatter.2.cloned.1.call-update) | async-done | bytes 524304 | tf_op jit(solution)/shard_map/reduce_scatter | solution.py:104
  133.0 23.0 %scatter_custom_fusion = bf16[1152,2048]{1,0:T(8,128)(2,1)} fusion(s32[1024]{0:T(1024)S(1)} %get-tuple-element.27, bf16[128,2048]{1,0:T(8,128)(2,1)S(1)} %fusion.31, s32[1024]{0:T(1024)S(1)} %get-tuple-element.26, bf16[]{:T(256)} %constant.82.clone.1), kind=kCustom, calls=%fused_computation.20 | custom fusion | bytes 4718594
  155.9 5.1 copy.98
  162.6 150.4 %all_to_all.19 = bf16[128,18,2048]{2,1,0:T(8,128)(2,1)} all-to-all(bf16[128,18,2048]{2,1,0:T(8,128)(2,1)S(1)} %bitcast.53), channel_id=1, replica_groups=mesh['req'=16,'exp'=8] {'req','exp'}, dimensions={0} | all-to-all | bytes 18874368 | tf_op jit(solution)/shard_map/all_to_all | solution.py:125
  313.0 14.1 %reshape.246 = bf16[2304,2048]{1,0:T(8,128)(2,1)} reshape(bf16[128,18,2048]{2,1,0:T(8,128)(2,1)} %all_to_all.19) | data formatting | bytes 18874368 | tf_op jit(solution)/shard_map/reshape | solution.py:127
  327.0 8.6 %fusion.20 = f32[2304,512]{1,0:T(8,128)S(1)} fusion(bf16[2304,2048]{1,0:T(8,128)(2,1)} %reshape.246, bf16[1,2048,512]{2,1,0:T(8,128)(2,1)} %param.25), kind=kOutput, calls=%fused_computation.33 | convolution fusion | flops 4831838208 | bytes 16252928 | tf_op jit(solution)/shard_map/dot_general | solution.py:128
  335.7 7.1 %fusion.7 = bf16[2304,512]{1,0:T(8,128)(2,1)} fusion(bf16[2304,2048]{1,0:T(8,128)(2,1)S(1)} %copy-done.2, f32[2304,512]{1,0:T(8,128)S(1)} %fusion.20, bf16[1,2048,512]{2,1,0:T(8,128)(2,1)S(1)} %copy-done.12), kind=kOutput, calls=%fused_computation.19 | convolution fusion | flops 4838916096 | bytes 18612224 | tf_op jit(solution)/shard_map/dot_general | solution.py:129
  342.7 4.9 dot_general.29
  347.6 7.3 %convolution_convert_fusion = bf16[128,18,2048]{2,0,1:T(8,128)(2,1)S(1)} fusion(bf16[128,18,512]{2,1,0:T(8,128)(2,1)} %dot_general.29, bf16[1,512,2048]{2,1,0:T(8,128)(2,1)S(1)} %copy-done), kind=kOutput, calls=%fused_computation.16 | convolution fusion | flops 4836556800 | bytes 13893632 | tf_op jit(solution)/shard_map/dot_general | solution.py:131
  354.9 20.9 %copy.100 = bf16[128,18,2048]{2,1,0:T(8,128)(2,1)} copy(bf16[128,18,2048]{2,0,1:T(8,128)(2,1)S(1)} %convolution_convert_fusion) | data formatting | bytes 18874368 | tf_op jit(solution)/shard_map/convert_element_type | solution.py:133
  375.8 10.1 %all-to-all-start.2 = ((bf16[128,18,2048]{2,1,0:T(8,128)(2,1)}), bf16[128,18,2048]{2,1,0:T(8,128)(2,1)}, u32[]{:S(2)}, u32[]{:S(2)}) async-start(bf16[128,18,2048]{2,1,0:T(8,128)(2,1)} %copy.100), calls=%async_computation.3 | async-start | bytes 25165824 | tf_op jit(solution)/shard_map/all_to_all | solution.py:132
  386.7 164.7 %all-to-all-done.2 = bf16[128,18,2048]{2,1,0:T(8,128)(2,1)} async-done(((bf16[128,18,2048]{2,1,0:T(8,128)(2,1)}), bf16[128,18,2048]{2,1,0:T(8,128)(2,1)}, u32[]{:S(2)}, u32[]{:S(2)}) %all-to-all-start.2) | async-done | bytes 9437216 | tf_op jit(solution)/shard_map/all_to_all | solution.py:132
  551.4 8.9 %bitcast_reduce_fusion = bf16[64,18,2048]{2,1,0:T(8,128)(2,1)S(1)} fusion(bf16[128,18,2048]{2,1,0:T(8,128)(2,1)} %all-to-all-done.2), kind=kLoop, calls=%fused_computation.9 | loop fusion | flops 2359296 | bytes 14155776 | tf_op jit(solution)/shard_map/reduce_sum | solution.py:140
  560.3 6.4 %copy_convert_fusion = f32[64,18,2048]{2,0,1:T(8,128)} fusion(bf16[64,18,2048]{2,1,0:T(8,128)(2,1)S(1)} %bitcast_reduce_fusion), kind=kLoop, calls=%fused_computation.18 | loop fusion | flops 2359296 | bytes 14155776 | tf_op jit(solution)/shard_map/convert_element_type | solution.py:142
  566.7 25.3 %gather_fusion.1 = f32[1024,2048]{1,0:T(8,128)} fusion(f32[64,18,2048]{2,0,1:T(8,128)} %copy_convert_fusion, s32[1024]{0:T(1024)S(1)} %bitcast.52), kind=kCustom, calls=%fused_computation.2 | custom fusion | bytes 16785408 | tf_op jit(solution)/shard_map/gather | solution.py:144
  592.0 6.6 %fusion.2 = f32[128,2048]{1,0:T(8,128)S(1)} fusion(f32[1024,2048]{1,0:T(8,128)} %gather_fusion.1, f32[128,8]{1,0:T(8,128)S(1)} %copy.102), kind=kLoop, calls=%fused_computation.11 | loop fusion | flops 3932160 | bytes 9441280 | tf_op jit(solution)/shard_map/reduce_sum | solution.py:145
  (84 shorter events, 41.2 us)
Async XLA Ops:
  6.5 341.1 %copy-start = (bf16[1,512,2048]{2,1,0:T(8,128)(2,1)S(1)}, bf16[1,512,2048]{2,1,0:T(8,128)(2,1)}, u32[]{:S(2)}) copy-start(bf16[1,512,2048]{2,1,0:T(8,128)(2,1)} %param.27) | copy-start | bytes 6291460
  6.5 17.9 %copy-start.13 = (s32[16]{0:T(128)S(1)}, s32[16]{0:T(128)}, u32[]{:S(2)}) copy-start(s32[16]{0:T(128)} %param.23) | copy-start | bytes 196
  6.5 38.0 %all-gather.2.cloned.1.call-start = ((), (), s32[]{:S(2)}) async-start(), calls=%async_computation.4 | async-start | bytes 4718592 | tf_op jit(solution)/shard_map/all_gather | solution.py:57
  17.0 21.9 %all-to-all-start = ((bf16[16,64,2,256]{3,2,1,0:T(2,128)(2,1)}), bf16[16,64,2,256]{3,2,1,0:T(2,128)(2,1)S(1)}, u32[]{:S(2)}, u32[]{:S(2)}) async-start(bf16[16,64,2,256]{3,2,1,0:T(2,128)(2,1)} %broadcast_select_fusion), calls=%async_computation | async-start | bytes 2097152 | tf_op jit(solution)/shard_map/all_to_all | solution.py:71
  24.2 106.2 %reduce-scatter.2.cloned.1.call-start = ((), (), s32[]{:S(2)}) async-start(), calls=%async_computation.5 | async-start | bytes 4718592 | tf_op jit(solution)/shard_map/reduce_scatter | solution.py:104
  69.0 10.8 %copy-start.5 = (bf16[1024,1,256]{0,2,1:T(8,128)(2,1)S(1)}, bf16[1024,1,256]{0,2,1:T(8,128)(2,1)}, u32[]{:S(2)}) copy-start(bf16[1024,1,256]{0,2,1:T(8,128)(2,1)} %copy.86) | copy-start | bytes 1572868
  69.0 10.8 %copy-start.6 = (bf16[1024,256]{0,1:T(8,128)(2,1)S(1)}, bf16[1024,256]{0,1:T(8,128)(2,1)}, u32[]{:S(2)}) copy-start(bf16[1024,256]{0,1:T(8,128)(2,1)} %slice.68) | copy-start | bytes 1572868
  79.9 8.9 %copy-start.4 = (bf16[256,2048]{1,0:T(8,128)(2,1)S(1)}, bf16[256,2048]{1,0:T(8,128)(2,1)}, u32[]{:S(2)}) copy-start(bf16[256,2048]{1,0:T(8,128)(2,1)} %param.20) | copy-start | bytes 3145732
  88.7 3.3 copy-start.8
  92.0 19.1 %copy-start.11 = (s32[2]{0:T(128)S(1)}, s32[2]{0:T(128)}, u32[]{:S(2)}) copy-start(s32[2]{0:T(128)} %constant.94) | copy-start | bytes 28
  92.0 19.2 %copy-start.10 = (s32[2]{0:T(128)S(1)}, s32[2]{0:T(128)}, u32[]{:S(2)}) copy-start(s32[2]{0:T(128)} %constant.97) | copy-start | bytes 28
  92.0 38.4 %copy-start.1 = (bf16[128,2048]{1,0:T(8,128)(2,1)S(1)}, bf16[128,2048]{1,0:T(8,128)(2,1)}, u32[]{:S(2)}) copy-start(bf16[128,2048]{1,0:T(8,128)(2,1)} %param.15) | copy-start | bytes 1572868
  92.0 39.7 %copy-start.7 = (f32[2048]{0:T(1024)S(1)}, f32[2048]{0:T(1024)}, u32[]{:S(2)}) copy-start(f32[2048]{0:T(1024)} %param.24) | copy-start | bytes 24580
  327.0 8.6 %copy-start.2 = (bf16[2304,2048]{1,0:T(8,128)(2,1)S(1)}, bf16[2304,2048]{1,0:T(8,128)(2,1)}, u32[]{:S(2)}) copy-start(bf16[2304,2048]{1,0:T(8,128)(2,1)} %reshape.246) | copy-start | bytes 28311556
  327.0 8.6 %copy-start.12 = (bf16[1,2048,512]{2,1,0:T(8,128)(2,1)S(1)}, bf16[1,2048,512]{2,1,0:T(8,128)(2,1)}, u32[]{:S(2)}) copy-start(bf16[1,2048,512]{2,1,0:T(8,128)(2,1)} %param.26) | copy-start | bytes 6291460
  375.8 10.1 %copy-start.9 = (f32[128,8]{0,1:T(8,128)S(1)}, f32[128,8]{0,1:T(8,128)}, u32[]{:S(2)}) copy-start(f32[128,8]{0,1:T(8,128)} %param.29) | copy-start | bytes 12292
  375.8 175.6 %all-to-all-start.2 = ((bf16[128,18,2048]{2,1,0:T(8,128)(2,1)}), bf16[128,18,2048]{2,1,0:T(8,128)(2,1)}, u32[]{:S(2)}, u32[]{:S(2)}) async-start(bf16[128,18,2048]{2,1,0:T(8,128)(2,1)} %copy.100), calls=%async_computation.3 | async-start | bytes 25165824 | tf_op jit(solution)/shard_map/all_to_all | solution.py:132
  592.0 6.6 %copy-start.3 = (bf16[128,2048]{1,0:T(8,128)(2,1)S(1)}, bf16[128,2048]{1,0:T(8,128)(2,1)}, u32[]{:S(2)}) copy-start(bf16[128,2048]{1,0:T(8,128)(2,1)} %reduce-scatter.2.cloned.1.call-done) | copy-start | bytes 1572868
Sparse Core Ops, SparseCore 0:
  10.1 34.3 all-gather.1
  92.1 38.1 reduce-scatter.1
where the time goes:
time: 612 us; the launch traced here: 607 us
  waiting for transfers between devices  195 us (32%)
  blocking collectives  150 us (25%)
  local copies, waits for them, and re-layouts  118 us (19%)
  other arithmetic  58.9 us (10%)
  matrix products  52.5 us (9%)
  starting transfers between devices  17.5 us (3%)
  between operations  14 us (2%)
    all_to_all x1, waiting for transfers between devices, on_device(): lax.all_to_all(part.reshape(senders, count, width).astype(jnp.bfloat16),...  165 us
    all_to_all x1, blocking collectives, on_device(): lax.all_to_all(doubled, ('req', 'exp'), split_axis=0, concat_axis=0, tile...  150 us
    unnamed x35, local copies, waits for them, and re-layouts  31.7 us
    gather x1, local copies, waits for them, and re-layouts, on_device(): picked = combined[flat, slot].reshape(rows_dev, top_count, width)  25.3 us
    another operation x3, other arithmetic  21.9 us
    convert_element_type x1, local copies, waits for them, and re-layouts, on_device(): part.reshape(senders, count, width).astype(jnp.bfloat16)  20.9 us
    reduce_scatter x1, waiting for transfers between devices, on_device(): lax.psum_scatter(jnp.dot(attn, w_out, preferred_element_type=jnp.float32)...  19.1 us
    reshape x1, local copies, waits for them, and re-layouts, on_device(): joined_rows = rows_in.reshape(senders * count, width)  14.1 us
  transfers between devices with their start and end apart: 4, of which 4 were waited for; matrix products, arithmetic and copies ran while one was open for 6% of the time, Pallas kernels for 0%

commit v1 on v0

--- a/solution.py
+++ b/solution.py
@@ -68,7 +68,10 @@
         jnp.bfloat16
     )
     outgoing = jnp.take(prefix_cache, group_of, axis=0)
-    arrived = lax.all_to_all(outgoing, "req", split_axis=0, concat_axis=1, tiled=True)[0]
+    arrived = jnp.concatenate(
+        lax.all_to_all(jnp.stack(jnp.split(outgoing, lax.axis_size("req"), axis=0)), "req", 0, 0),
+        axis=1,
+    )[0]
     prefix_len = arrived.shape[0]
     query = projected[:, :local_width].reshape(slot_count, local_heads, head_dim)
     keys = jnp.concatenate(

time: 612 us -> 622 us (1.016)
  local copies, waits for them, and re-layouts: 118 us -> 129 us
    unnamed x35 -> x50, local copies, waits for them, and re-layouts: 31.7 us -> 41.7 us
  transfers between devices with their start and end apart: 4 -> 4, of which waited for: 4 -> 3; matrix products, arithmetic and copies ran while one was open for 6% -> 7% of each run, Pallas kernels for 0% -> 0%
where the time goes in v1:
time: 622 us; the launch traced here: 616 us
  waiting for transfers between devices  195 us (31%)
  blocking collectives  150 us (24%)
  local copies, waits for them, and re-layouts  129 us (21%)
  other arithmetic  57.9 us (9%)
  matrix products  52.5 us (8%)
  starting transfers between devices  17.5 us (3%)
  between operations  14 us (2%)
    all_to_all x1, waiting for transfers between devices, on_device(): lax.all_to_all(part.reshape(senders, count, width).astype(jnp.bfloat16),...  165 us
    all_to_all x1, blocking collectives, on_device(): lax.all_to_all(doubled, ('req', 'exp'), split_axis=0, concat_axis=0, tile...  150 us
    unnamed x50, local copies, waits for them, and re-layouts  41.7 us
    gather x1, local copies, waits for them, and re-layouts, on_device(): picked = combined[flat, slot].reshape(rows_dev, top_count, width)  25.3 us
    another operation x3, other arithmetic  21.9 us
    convert_element_type x1, local copies, waits for them, and re-layouts, on_device(): part.reshape(senders, count, width).astype(jnp.bfloat16)  20.9 us
    reduce_scatter x1, waiting for transfers between devices, on_device(): lax.psum_scatter(jnp.dot(attn, w_out, preferred_element_type=jnp.float32)...  20.3 us
    reshape x1, local copies, waits for them, and re-layouts, on_device(): joined_rows = rows_in.reshape(senders * count, width)  14.1 us
  transfers between devices with their start and end apart: 4, of which 3 were waited for; matrix products, arithmetic and copies ran while one was open for 7% of the time, Pallas kernels for 0%

profile of v1, /device:TPU:24, one launch (start us, length us, event | category | flops | bytes accessed | tf_op | source)
XLA Modules:
  0.0 616.3 jit_solution(3637615925226559148)
XLA Ops:
  10.7 3.7 gather_fusion
  26.6 7.2 %all-to-all-start = ((bf16[16,1,64,2,256]{4,3,2,1,0:T(2,128)(2,1)}), bf16[16,1,64,2,256]{4,3,2,1,0:T(2,128)(2,1)S(1)}, u32[]{:S(2)}, u32[]{:S(2)}) async-start(bf16[16,1,64,2,256]{4,3,2,1,0:T(2,128)(2,1)} %fusion.41), calls=%async_computation | async-start | bytes 2097152 | tf_op jit(solution)/shard_map/all_to_all | solution.py:72
  38.4 10.1 %all-to-all-done = bf16[16,1,64,2,256]{4,3,2,1,0:T(2,128)(2,1)S(1)} async-done(((bf16[16,1,64,2,256]{4,3,2,1,0:T(2,128)(2,1)}), bf16[16,1,64,2,256]{4,3,2,1,0:T(2,128)(2,1)S(1)}, u32[]{:S(2)}, u32[]{:S(2)}) %all-to-all-start) | async-done | bytes 1048608 | tf_op jit(solution)/shard_map/all_to_all | solution.py:72
  52.9 6.7 %fusion.10 = f32[1024,768]{0,1:T(8,128)S(1)} fusion(bf16[1024,2048]{1,0:T(8,128)(2,1)} %all-gather.2.cloned.1.call-done, bf16[2048,256]{1,0:T(8,128)(2,1)} %param.19, bf16[2048,256]{1,0:T(8,128)(2,1)} %param.18, bf16[2048,256]{1,0:T(8,128)(2,1)} %param.17), kind=kOutput, calls=%fused_computation.23 | convolution fusion | flops 3230662656 | bytes 10485760 | tf_op jit(solution)/shard_map/dot_general | solution.py:59
  73.5 3.9 subtract_convert_fusion.1
  77.4 10.8 %fusion.69 = (f32[2,1024]{1,0:T(2,128)S(1)}, f32[2,1024,2048]{2,1,0:T(8,128)}) fusion(pred[2048]{0:T(1024)(128)(4,1)S(1)} %concatenate.28, bf16[1024,2,64]{2,0,1:T(8,128)(2,1)} %get-tuple-element.13, bf16[1024,2,64]{2,0,1:T(8,128)(2,1)} %get-tuple-element.14, bf16[1024,2,128]{2,0,1:T(8,128)(2,1)} %copy.107, bf16[1024,2,64]{2,0,1:T(8,128)(2,1)} %get-tuple-element.6, ...), kind=kOutput, calls=%fused_computation.137 | convolution fusion | flops 1094715392 | bytes 18360320 | tf_op jit(solution)/shard_map/sub | solution.py:100
  88.3 8.8 %fusion.24 = bf16[2,128,1024]{2,1,0:T(8,128)(2,1)S(1)} fusion(f32[2,1024,2048]{2,1,0:T(8,128)} %get-tuple-element.25, f32[2,1024]{1,0:T(2,128)S(1)} %get-tuple-element.24, bf16[1024,2,128]{0,2,1:T(8,128)(2,1)S(1)} %bitcast.126, bf16[1024,2,128]{0,2,1:T(8,128)(2,1)S(1)} %bitcast.125), kind=kOutput, calls=%fused_computation.43 | convolution fusion | flops 1084489728 | bytes 18358272 | tf_op jit(solution)/shard_map/hqk,khd->qhd/dot_general | solution.py:103
  100.8 18.0 %reduce-window.6 = s32[64,8,128]{2,1,0:T(8,128)S(1)} reduce-window(s32[64,8,128]{2,1,0:T(8,128)S(1)} %fusion.39, s32[]{:T(128)} %constant.39.clone.1), window={size=1x1x128 pad=0_0x0_0x127_0}, to_apply=%region_4.5 | reduce-window | flops 8323072 | bytes 524292 | tf_op jit(solution)/shard_map/reduce-window
  119.7 20.3 %reduce-scatter.2.cloned.1.call-done = bf16[128,2048]{1,0:T(8,128)(2,1)} async-done(((bf16[1024,2048]{1,0:T(8,128)(2,1)}), bf16[128,2048]{1,0:T(8,128)(2,1)}) %reduce-scatter.2.cloned.1.call-update) | async-done | bytes 524304 | tf_op jit(solution)/shard_map/reduce_scatter | solution.py:107
  142.6 23.0 %scatter_custom_fusion = bf16[1152,2048]{1,0:T(8,128)(2,1)} fusion(s32[1024]{0:T(1024)S(1)} %get-tuple-element.27, bf16[128,2048]{1,0:T(8,128)(2,1)S(1)} %fusion.31, s32[1024]{0:T(1024)S(1)} %get-tuple-element.26, bf16[]{:T(256)} %constant.82.clone.1), kind=kCustom, calls=%fused_computation.20 | custom fusion | bytes 4718594
  165.6 5.1 copy.113
  172.2 150.4 %all_to_all.15 = bf16[128,18,2048]{2,1,0:T(8,128)(2,1)} all-to-all(bf16[128,18,2048]{2,1,0:T(8,128)(2,1)S(1)} %bitcast.117), channel_id=1, replica_groups=mesh['req'=16,'exp'=8] {'req','exp'}, dimensions={0} | all-to-all | bytes 18874368 | tf_op jit(solution)/shard_map/all_to_all | solution.py:128
  322.6 14.1 %reshape.242 = bf16[2304,2048]{1,0:T(8,128)(2,1)} reshape(bf16[128,18,2048]{2,1,0:T(8,128)(2,1)} %all_to_all.15) | data formatting | bytes 18874368 | tf_op jit(solution)/shard_map/reshape | solution.py:130
  336.7 8.6 %fusion.20 = f32[2304,512]{1,0:T(8,128)S(1)} fusion(bf16[2304,2048]{1,0:T(8,128)(2,1)} %reshape.242, bf16[1,2048,512]{2,1,0:T(8,128)(2,1)} %param.25), kind=kOutput, calls=%fused_computation.33 | convolution fusion | flops 4831838208 | bytes 16252928 | tf_op jit(solution)/shard_map/dot_general | solution.py:131
  345.3 7.1 %fusion.7 = bf16[2304,512]{1,0:T(8,128)(2,1)} fusion(bf16[2304,2048]{1,0:T(8,128)(2,1)S(1)} %copy-done.2, f32[2304,512]{1,0:T(8,128)S(1)} %fusion.20, bf16[1,2048,512]{2,1,0:T(8,128)(2,1)S(1)} %copy-done.12), kind=kOutput, calls=%fused_computation.19 | convolution fusion | flops 4838916096 | bytes 18612224 | tf_op jit(solution)/shard_map/dot_general | solution.py:132
  352.4 4.9 dot_general.29
  357.2 7.3 %convolution_convert_fusion = bf16[128,18,2048]{2,0,1:T(8,128)(2,1)S(1)} fusion(bf16[128,18,512]{2,1,0:T(8,128)(2,1)} %dot_general.29, bf16[1,512,2048]{2,1,0:T(8,128)(2,1)S(1)} %copy-done), kind=kOutput, calls=%fused_computation.16 | convolution fusion | flops 4836556800 | bytes 13893632 | tf_op jit(solution)/shard_map/dot_general | solution.py:134
  364.5 20.9 %copy.115 = bf16[128,18,2048]{2,1,0:T(8,128)(2,1)} copy(bf16[128,18,2048]{2,0,1:T(8,128)(2,1)S(1)} %convolution_convert_fusion) | data formatting | bytes 18874368 | tf_op jit(solution)/shard_map/convert_element_type | solution.py:136
  385.5 10.1 %all-to-all-start.2 = ((bf16[128,18,2048]{2,1,0:T(8,128)(2,1)}), bf16[128,18,2048]{2,1,0:T(8,128)(2,1)}, u32[]{:S(2)}, u32[]{:S(2)}) async-start(bf16[128,18,2048]{2,1,0:T(8,128)(2,1)} %copy.115), calls=%async_computation.3 | async-start | bytes 25165824 | tf_op jit(solution)/shard_map/all_to_all | solution.py:135
  396.3 164.7 %all-to-all-done.2 = bf16[128,18,2048]{2,1,0:T(8,128)(2,1)} async-done(((bf16[128,18,2048]{2,1,0:T(8,128)(2,1)}), bf16[128,18,2048]{2,1,0:T(8,128)(2,1)}, u32[]{:S(2)}, u32[]{:S(2)}) %all-to-all-start.2) | async-done | bytes 9437216 | tf_op jit(solution)/shard_map/all_to_all | solution.py:135
  561.0 8.9 %bitcast_reduce_fusion = bf16[64,18,2048]{2,1,0:T(8,128)(2,1)S(1)} fusion(bf16[128,18,2048]{2,1,0:T(8,128)(2,1)} %all-to-all-done.2), kind=kLoop, calls=%fused_computation.9 | loop fusion | flops 2359296 | bytes 14155776 | tf_op jit(solution)/shard_map/reduce_sum | solution.py:143
  569.9 6.4 %copy_convert_fusion = f32[64,18,2048]{2,0,1:T(8,128)} fusion(bf16[64,18,2048]{2,1,0:T(8,128)(2,1)S(1)} %bitcast_reduce_fusion), kind=kLoop, calls=%fused_computation.18 | loop fusion | flops 2359296 | bytes 14155776 | tf_op jit(solution)/shard_map/convert_element_type | solution.py:145
  576.3 25.3 %gather_fusion.1 = f32[1024,2048]{1,0:T(8,128)} fusion(f32[64,18,2048]{2,0,1:T(8,128)} %copy_convert_fusion, s32[1024]{0:T(1024)S(1)} %bitcast.116), kind=kCustom, calls=%fused_computation.2 | custom fusion | bytes 16785408 | tf_op jit(solution)/shard_map/gather | solution.py:147
  601.6 6.6 %fusion.2 = f32[128,2048]{1,0:T(8,128)S(1)} fusion(f32[1024,2048]{1,0:T(8,128)} %gather_fusion.1, f32[128,8]{1,0:T(8,128)S(1)} %copy.117), kind=kLoop, calls=%fused_computation.11 | loop fusion | flops 3932160 | bytes 9441280 | tf_op jit(solution)/shard_map/reduce_sum | solution.py:148
  (100 shorter events, 49.6 us)
Async XLA Ops:
  6.5 350.7 %copy-start = (bf16[1,512,2048]{2,1,0:T(8,128)(2,1)S(1)}, bf16[1,512,2048]{2,1,0:T(8,128)(2,1)}, u32[]{:S(2)}) copy-start(bf16[1,512,2048]{2,1,0:T(8,128)(2,1)} %param.27) | copy-start | bytes 6291460
  6.5 46.4 %all-gather.2.cloned.1.call-start = ((), (), s32[]{:S(2)}) async-start(), calls=%async_computation.4 | async-start | bytes 4718592 | tf_op jit(solution)/shard_map/all_gather | solution.py:57
  10.0 24.1 %copy-start.13 = (s32[16]{0:T(128)S(1)}, s32[16]{0:T(128)}, u32[]{:S(2)}) copy-start(s32[16]{0:T(128)} %param.23) | copy-start | bytes 196
  26.6 21.9 %all-to-all-start = ((bf16[16,1,64,2,256]{4,3,2,1,0:T(2,128)(2,1)}), bf16[16,1,64,2,256]{4,3,2,1,0:T(2,128)(2,1)S(1)}, u32[]{:S(2)}, u32[]{:S(2)}) async-start(bf16[16,1,64,2,256]{4,3,2,1,0:T(2,128)(2,1)} %fusion.41), calls=%async_computation | async-start | bytes 2097152 | tf_op jit(solution)/shard_map/all_to_all | solution.py:72
  33.8 106.2 %reduce-scatter.2.cloned.1.call-start = ((), (), s32[]{:S(2)}) async-start(), calls=%async_computation.5 | async-start | bytes 4718592 | tf_op jit(solution)/shard_map/reduce_scatter | solution.py:107
  77.4 10.8 %copy-start.5 = (bf16[1024,1,256]{0,2,1:T(8,128)(2,1)S(1)}, bf16[1024,1,256]{0,2,1:T(8,128)(2,1)}, u32[]{:S(2)}) copy-start(bf16[1024,1,256]{0,2,1:T(8,128)(2,1)} %copy.101) | copy-start | bytes 1572868
  77.4 10.8 %copy-start.6 = (bf16[1024,256]{0,1:T(8,128)(2,1)S(1)}, bf16[1024,256]{0,1:T(8,128)(2,1)}, u32[]{:S(2)}) copy-start(bf16[1024,256]{0,1:T(8,128)(2,1)} %slice.68) | copy-start | bytes 1572868
  88.3 8.9 %copy-start.4 = (bf16[256,2048]{1,0:T(8,128)(2,1)S(1)}, bf16[256,2048]{1,0:T(8,128)(2,1)}, u32[]{:S(2)}) copy-start(bf16[256,2048]{1,0:T(8,128)(2,1)} %param.20) | copy-start | bytes 3145732
  97.1 3.3 copy-start.8
  100.4 19.1 %copy-start.11 = (s32[2]{0:T(128)S(1)}, s32[2]{0:T(128)}, u32[]{:S(2)}) copy-start(s32[2]{0:T(128)} %constant.94) | copy-start | bytes 28
  100.4 19.2 %copy-start.10 = (s32[2]{0:T(128)S(1)}, s32[2]{0:T(128)}, u32[]{:S(2)}) copy-start(s32[2]{0:T(128)} %constant.97) | copy-start | bytes 28
  100.4 39.6 %copy-start.1 = (bf16[128,2048]{1,0:T(8,128)(2,1)S(1)}, bf16[128,2048]{1,0:T(8,128)(2,1)}, u32[]{:S(2)}) copy-start(bf16[128,2048]{1,0:T(8,128)(2,1)} %param.15) | copy-start | bytes 1572868
  100.4 41.0 %copy-start.7 = (f32[2048]{0:T(1024)S(1)}, f32[2048]{0:T(1024)}, u32[]{:S(2)}) copy-start(f32[2048]{0:T(1024)} %param.24) | copy-start | bytes 24580
  336.7 8.6 %copy-start.2 = (bf16[2304,2048]{1,0:T(8,128)(2,1)S(1)}, bf16[2304,2048]{1,0:T(8,128)(2,1)}, u32[]{:S(2)}) copy-start(bf16[2304,2048]{1,0:T(8,128)(2,1)} %reshape.242) | copy-start | bytes 28311556
  336.7 8.6 %copy-start.12 = (bf16[1,2048,512]{2,1,0:T(8,128)(2,1)S(1)}, bf16[1,2048,512]{2,1,0:T(8,128)(2,1)}, u32[]{:S(2)}) copy-start(bf16[1,2048,512]{2,1,0:T(8,128)(2,1)} %param.26) | copy-start | bytes 6291460
  385.5 10.1 %copy-start.9 = (f32[128,8]{0,1:T(8,128)S(1)}, f32[128,8]{0,1:T(8,128)}, u32[]{:S(2)}) copy-start(f32[128,8]{0,1:T(8,128)} %param.29) | copy-start | bytes 12292
  385.5 175.6 %all-to-all-start.2 = ((bf16[128,18,2048]{2,1,0:T(8,128)(2,1)}), bf16[128,18,2048]{2,1,0:T(8,128)(2,1)}, u32[]{:S(2)}, u32[]{:S(2)}) async-start(bf16[128,18,2048]{2,1,0:T(8,128)(2,1)} %copy.115), calls=%async_computation.3 | async-start | bytes 25165824 | tf_op jit(solution)/shard_map/all_to_all | solution.py:135
  601.6 6.6 %copy-start.3 = (bf16[128,2048]{1,0:T(8,128)(2,1)S(1)}, bf16[128,2048]{1,0:T(8,128)(2,1)}, u32[]{:S(2)}) copy-start(bf16[128,2048]{1,0:T(8,128)(2,1)} %reduce-scatter.2.cloned.1.call-done) | copy-start | bytes 1572868
Sparse Core Ops, SparseCore 0:
  10.1 34.3 all-gather.1
  100.5 39.4 reduce-scatter.1
